TPU v7x, 32 devices: a whole 2x2x4 slice. The times are simulated.
32 devices in a mesh: dp: 4 (over y, core), row: 2 (over x), col: 4 (over z).
Axes of the slice: x: 2, y: 2, z: 4, core: 2. Of those that a mesh axis runs over, the one named last changes fastest.
Arguments:
- tokens: bfloat16 [8192, 1024], P(('dp', 'row'), 'col'), may hold values from -6 to 6
- passages: bfloat16 [32, 300, 1024], P(('dp', 'row'), None, 'col'), may hold values from -6 to 6
- lengths: int32 [8], replicated, may hold values from 256 to 1792, as said below
- block_order: int32 [64], replicated, may hold values from 0 to 63, as said below
- passage_ids: int32 [8, 5], replicated, may hold values from 0 to 31, as said below
- triple_weight: bfloat16 [1024, 3, 1024], P('col', None, 'row'), may hold values from -0.1875 to 0.1875
- self_out_weight: bfloat16 [1024, 1024], P('row', 'col'), may hold values from -2 to 2
- query_weight: bfloat16 [1024, 1, 1024], P('col', None, 'row'), may hold values from -0.1875 to 0.1875
- memory_weight: bfloat16 [1024, 2, 1024], P('col', None, 'row'), may hold values from -0.1875 to 0.1875
- cross_out_weight: bfloat16 [1024, 1024], P('row', 'col'), may hold values from -4 to 4
- expand_weight: bfloat16 [1024, 1, 4096], P('col', None, 'row'), may hold values from -0.1875 to 0.1875
- contract_weight: bfloat16 [4096, 1024], P('row', 'col'), may hold values from -0.09375 to 0.09375
- norm_gain: bfloat16 [3, 1024], P(None, 'col'), may hold values from 0.25 to 1.75
- norm_bias: bfloat16 [3, 1024], P(None, 'col'), may hold values from -1.5 to 1.5
- cotangent: bfloat16 [8192, 1024], P(('dp', 'row'), 'col'), may hold values from -6 to 6
Outputs:
- output: bfloat16 [8192, 1024], P(('dp', 'row'), 'col')
- grad_tokens: bfloat16 [8192, 1024], P(('dp', 'row'), 'col')
- grad_passages: bfloat16 [32, 300, 1024], P(('dp', 'row'), None, 'col')
- grad_triple: float32 [1024, 3, 1024], P('col', None, 'row')
- grad_self_out: float32 [1024, 1024], P('row', 'col')
- grad_query: float32 [1024, 1, 1024], P('col', None, 'row')
- grad_memory: float32 [1024, 2, 1024], P('col', None, 'row')
- grad_cross_out: float32 [1024, 1024], P('row', 'col')
- grad_expand: float32 [1024, 1, 4096], P('col', None, 'row')
- grad_contract: float32 [4096, 1024], P('row', 'col')
- grad_norm_gain: float32 [3, 1024], P(None, 'col')
- grad_norm_bias: float32 [3, 1024], P(None, 'col')
Inputs may be any that keep to these rules, and one draw needn't show every extreme that they name: For every group g the lengths 2g and 2g + 1 sum to 2048; some group holds a sequence of exactly 256 tokens. `block_order`: A permutation of the blocks that keeps every block at its index of row: the block of group order q = (g * 2 + r) * 8 + j comes from a given-order block with the same r. The blocks of one index of dp and row in given order go to exactly 2 groups, 4 to each, and the blocks of one index of dp and row in group order come from exactly 2 groups, 4 from each. `passage_ids`: each sequence names 5 different passages of its own group's pool (g * 8 to (g + 1) * 8 - 1 for group g), and each passage of a pool is named by one of the group's two sequences.
All inputs are finite; a program needn't handle non-finite values.
Results may differ from a plain program's by a relative error of at most 0.03.
Values may be sent and summed in bfloat16 or wider, within the bound.
No kernel may reach another device: no remote copies, remote signals or barrier semaphores. Data moves between devices by JAX's collectives and lax.ppermute only.
A program may use at most 192 MiB of HBM per device.

v0:
```python
import jax
import jax.numpy as jnp
from jax import lax
from jax.sharding import PartitionSpec as P

HD = 64
PLEN = 300
TOPP = 5
PP_GRP = 8
BLK = 128


epsilon = 1e-05
masked_out = -1000000000.0


def self_mask(first, total):

    def allowed(start, count):
        query_pos = start + jnp.arange(count, dtype=jnp.int32)
        key_pos = jnp.arange(total, dtype=jnp.int32)
        begin = jnp.where(query_pos >= first, first, 0)
        return (key_pos[None, :] <= query_pos[:, None]) & (key_pos[None, :] >= begin[:, None])

    return allowed


def cross_mask(first, chosen_ids, key_count):
    key_passage = jnp.arange(key_count, dtype=jnp.int32) // PLEN
    member = jnp.any(key_passage[None, None, :] == chosen_ids[:, :, None], 1)

    def allowed(start, count):
        query_pos = start + jnp.arange(count, dtype=jnp.int32)
        later = (query_pos >= first)[:, None]
        return jnp.where(later, member[1][None, :], member[0][None, :])

    return allowed


def regroup(pair, select, placing, groups):
    width = pair[0].shape[-1]
    first_out = pair[0].reshape(-1, BLK, width)[select].reshape(groups, -1, width)
    second_out = pair[1].reshape(-1, BLK, width)[select].reshape(groups, -1, width)
    moved = (
        lax.all_to_all(first_out, "dp", split_axis=0, concat_axis=0, tiled=True),
        lax.all_to_all(second_out, "dp", split_axis=0, concat_axis=0, tiled=True),
    )
    return tuple((arrived.reshape(-1, BLK, width)[placing].reshape(-1, width) for arrived in moved))


def project_in(rows_low, weight):
    gathered = lax.all_gather(rows_low, "row", axis=0, tiled=True)
    partial_sum = jnp.einsum("rf,fke->rke", gathered, weight, preferred_element_type=jnp.float32)
    result = lax.psum_scatter(partial_sum, "col", scatter_dimension=2, tiled=True)
    return (gathered, result)


def project_in_back(gathered, weight, grad_low):
    wide = lax.all_gather(grad_low, "col", axis=2, tiled=True)
    grad_weight = jnp.einsum("rf,rke->fke", gathered, wide, preferred_element_type=jnp.float32)

    def term(start, count):
        return jnp.einsum("rke,fke->rf", wide, weight, preferred_element_type=jnp.float32)

    grad_rows = lax.psum_scatter(
        term(
            jnp.int32(0), lax.axis_size("row") * (gathered.shape[0] // lax.axis_size("row"))
        ).astype(jnp.bfloat16),
        "row",
        scatter_dimension=0,
        tiled=True,
    ).astype(jnp.float32)
    return (grad_weight, grad_rows)


def project_out(heads_low, weight):
    wide = lax.all_gather(heads_low, "col", axis=1, tiled=True)

    def term(start, count):
        return jnp.dot(wide, weight, preferred_element_type=jnp.float32)

    own = lax.psum_scatter(
        term(jnp.int32(0), wide.shape[0] // lax.axis_size("row") * lax.axis_size("row")),
        "row",
        scatter_dimension=0,
        tiled=True,
    )
    return (wide, own)


def project_out_back(wide, weight, grad_low):
    tall = lax.all_gather(grad_low, "row", axis=0, tiled=True)
    grad_weight = jnp.einsum("re,rf->ef", wide, tall, preferred_element_type=jnp.float32)
    partial_sum = jnp.einsum("rf,ef->re", tall, weight, preferred_element_type=jnp.float32)
    grad_heads = lax.psum_scatter(
        partial_sum.astype(jnp.bfloat16), "col", scatter_dimension=1, tiled=True
    ).astype(jnp.float32)
    return (grad_weight, grad_heads)


def row_sums(first_terms, second_terms):
    return lax.psum((jnp.sum(first_terms, 1), jnp.sum(second_terms, 1)), "col")


def norm_forward(value, gain, offset, features):
    total, squares = row_sums(value, value * value)
    center = total / features
    spread = squares / features - center * center
    scale = lax.rsqrt(spread + epsilon)
    normed = (value - center[:, None]) * scale[:, None]
    return (normed * gain + offset, normed, scale)


def norm_back(grad, normed, scale, gain, features):
    scaled = grad * gain
    total, crossed = row_sums(scaled, scaled * normed)
    grad_value = scale[:, None] * (
        scaled - total[:, None] / features - normed * crossed[:, None] / features
    )
    return (grad_value, jnp.sum(grad * normed, 0), jnp.sum(grad, 0))


def attend(queries, keys, values, allowed):
    total = queries.shape[0]
    block = min(512, total)
    factor = queries.shape[-1] ** (-0.5)

    def one_block(index):
        start = index * block
        chosen = lax.dynamic_slice_in_dim(queries, start, block, 0)
        scores = (
            jnp.einsum("qhe,khe->hqk", chosen, keys, preferred_element_type=jnp.float32) * factor
        )
        scores = jnp.where(allowed(start, block)[None], scores, masked_out)
        top = jnp.max(scores, -1, keepdims=True)
        expo = jnp.exp(scores - top)
        summed = jnp.sum(expo, -1, keepdims=True)
        probs = (expo / summed).astype(jnp.bfloat16)
        result = jnp.einsum(
            "hqk,khe->qhe", probs, values, preferred_element_type=jnp.float32
        ).astype(jnp.bfloat16)
        return (result, (top + jnp.log(summed))[..., 0])

    outputs, log_totals = lax.map(one_block, jnp.arange(total // block, dtype=jnp.int32))
    return (outputs.reshape(queries.shape), log_totals)


def attend_back(queries, keys, values, log_totals, grad_out, allowed):
    total = queries.shape[0]
    block = min(512, total)
    factor = queries.shape[-1] ** (-0.5)

    def one_block(carry, item):
        grad_keys, grad_values = carry
        index, lse_block = item
        start = index * block
        chosen = lax.dynamic_slice_in_dim(queries, start, block, 0)
        upper = lax.dynamic_slice_in_dim(grad_out, start, block, 0)
        scores = (
            jnp.einsum("qhe,khe->hqk", chosen, keys, preferred_element_type=jnp.float32) * factor
        )
        scores = jnp.where(allowed(start, block)[None], scores, masked_out)
        probs = jnp.exp(scores - lse_block[:, :, None])
        grad_values = grad_values + jnp.einsum(
            "hqk,qhe->khe", probs.astype(jnp.bfloat16), upper, preferred_element_type=jnp.float32
        )
        grad_probs = jnp.einsum("qhe,khe->hqk", upper, values, preferred_element_type=jnp.float32)
        inner = jnp.sum(grad_probs * probs, -1, keepdims=True)
        grad_scores = (probs * (grad_probs - inner)).astype(jnp.bfloat16)
        grad_queries = (
            jnp.einsum("hqk,khe->qhe", grad_scores, keys, preferred_element_type=jnp.float32)
            * factor
        )
        grad_keys = (
            grad_keys
            + jnp.einsum("hqk,qhe->khe", grad_scores, chosen, preferred_element_type=jnp.float32)
            * factor
        )
        return ((grad_keys, grad_values), grad_queries)

    zeros = jnp.zeros(keys.shape, jnp.float32)
    steps = jnp.arange(total // block, dtype=jnp.int32)
    (grad_keys, grad_values), grad_queries = lax.scan(
        one_block, (zeros, zeros), (steps, log_totals)
    )
    return (grad_queries.reshape(queries.shape), grad_keys, grad_values)


def gelu_exact(value):
    return jax.nn.gelu(value, approximate=False)


def on_device(
    tokens,
    passages,
    lengths,
    block_order,
    passage_ids,
    triple_weight,
    self_out_weight,
    query_weight,
    memory_weight,
    cross_out_weight,
    expand_weight,
    contract_weight,
    norm_gain,
    norm_bias,
    cotangent,
):
    groups = lax.axis_size("dp")
    row_count = lax.axis_size("row")
    col_count = lax.axis_size("col")
    group = lax.axis_index("dp")
    row_index = lax.axis_index("row")
    own_rows, width = tokens.shape
    features = width * col_count
    blocks = own_rows // BLK
    capacity = blocks // (groups // 2)
    span = row_count * blocks
    all_blocks = block_order.shape[0]
    block_ids = jnp.arange(blocks, dtype=jnp.int32)
    slot_ids = jnp.arange(groups * capacity, dtype=jnp.int32)
    inverse = (
        jnp.zeros_like(block_order).at[block_order].set(jnp.arange(all_blocks, dtype=jnp.int32))
    )
    own_blocks = (group * row_count + row_index) * blocks + block_ids
    target = inverse[own_blocks] // span
    earlier = block_ids[None, :] < block_ids[:, None]
    ranking = jnp.sum((target[None, :] == target[:, None]) & earlier, 1)
    matches = (target[None, :] == (slot_ids // capacity)[:, None]) & (
        ranking[None, :] == (slot_ids % capacity)[:, None]
    )
    send_select = jnp.sum(jnp.where(matches, block_ids[None, :], 0), 1)
    back_place = target * capacity + ranking
    wanted = block_order[own_blocks]
    source = wanted // span
    within = wanted % blocks
    rank_in = jnp.sum((source[None, :] == source[:, None]) & (within[None, :] < within[:, None]), 1)
    recv_place = source * capacity + rank_in
    back_matches = recv_place[None, :] == slot_ids[:, None]
    back_select = jnp.sum(jnp.where(back_matches, block_ids[None, :], 0), 1)
    inputs, upstream = regroup((tokens, cotangent), send_select, recv_place, groups)
    total = own_rows * row_count
    pair_len = lax.dynamic_slice_in_dim(lengths, group * 2, 2)
    first = pair_len[0]
    chosen_ids = lax.dynamic_slice(passage_ids, (group * 2, 0), (2, TOPP)) - group * PP_GRP
    gains = norm_gain.astype(jnp.float32)
    offsets = norm_bias.astype(jnp.float32)
    head_width = triple_weight.shape[2] // col_count
    head_count = head_width // HD
    own_mask = self_mask(first, total)
    feats = inputs.astype(jnp.float32)
    input_rows, triple = project_in(inputs, triple_weight)
    triple = triple.astype(jnp.bfloat16).reshape(total, 3, head_count, HD)
    attended, self_lse = attend(triple[:, 0], triple[:, 1], triple[:, 2], own_mask)
    self_wide, self_branch = project_out(attended.reshape(total, head_width), self_out_weight)
    normed_one, keep_one, scale_one = norm_forward(
        feats + self_branch, gains[0], offsets[0], features
    )
    one_rows, queries = project_in(normed_one.astype(jnp.bfloat16), query_weight)
    queries = queries.astype(jnp.bfloat16).reshape(total, head_count, HD)
    memory_rows, pairs = project_in(passages.reshape(-1, width), memory_weight)
    key_count = memory_rows.shape[0]
    pairs = pairs.astype(jnp.bfloat16).reshape(key_count, 2, head_count, HD)
    other_mask = cross_mask(first, chosen_ids, key_count)
    crossed, cross_lse = attend(queries, pairs[:, 0], pairs[:, 1], other_mask)
    cross_wide, cross_branch = project_out(crossed.reshape(total, head_width), cross_out_weight)
    normed_two, keep_two, scale_two = norm_forward(
        normed_one + cross_branch, gains[1], offsets[1], features
    )
    two_rows, hidden = project_in(normed_two.astype(jnp.bfloat16), expand_weight)
    active, gelu_pull = jax.vjp(gelu_exact, hidden[:, 0])
    ffn_wide, ffn_branch = project_out(active.astype(jnp.bfloat16), contract_weight)
    final, keep_three, scale_three = norm_forward(
        normed_two + ffn_branch, gains[2], offsets[2], features
    )
    grad_three, gain_three, bias_three = norm_back(
        upstream.astype(jnp.float32), keep_three, scale_three, gains[2], features
    )
    contract_grad, grad_active = project_out_back(
        ffn_wide, contract_weight, grad_three.astype(jnp.bfloat16)
    )
    grad_hidden = gelu_pull(grad_active)[0].astype(jnp.bfloat16)
    expand_grad, grad_two_in = project_in_back(two_rows, expand_weight, grad_hidden[:, None])
    grad_two, gain_two, bias_two = norm_back(
        grad_three + grad_two_in, keep_two, scale_two, gains[1], features
    )
    cross_out_grad, grad_crossed = project_out_back(
        cross_wide, cross_out_weight, grad_two.astype(jnp.bfloat16)
    )
    grad_crossed = grad_crossed.astype(jnp.bfloat16).reshape(total, head_count, HD)
    grad_queries, grad_keys, grad_values = attend_back(
        queries, pairs[:, 0], pairs[:, 1], cross_lse, grad_crossed, other_mask
    )
    query_grad, grad_one_in = project_in_back(
        one_rows, query_weight, grad_queries.astype(jnp.bfloat16).reshape(total, 1, head_width)
    )
    stacked = (
        jnp.stack([grad_keys, grad_values], 1)
        .astype(jnp.bfloat16)
        .reshape(key_count, 2, head_width)
    )
    memory_grad, grad_memory_rows = project_in_back(memory_rows, memory_weight, stacked)
    grad_one, gain_one, bias_one = norm_back(
        grad_two + grad_one_in, keep_one, scale_one, gains[0], features
    )
    self_out_grad, grad_attended = project_out_back(
        self_wide, self_out_weight, grad_one.astype(jnp.bfloat16)
    )
    grad_attended = grad_attended.astype(jnp.bfloat16).reshape(total, head_count, HD)
    grad_first, grad_second, grad_third = attend_back(
        triple[:, 0], triple[:, 1], triple[:, 2], self_lse, grad_attended, own_mask
    )
    grad_triple_all = (
        jnp.stack([grad_first, grad_second, grad_third], 1)
        .astype(jnp.bfloat16)
        .reshape(total, 3, head_width)
    )
    triple_grad, grad_input_in = project_in_back(input_rows, triple_weight, grad_triple_all)
    grad_inputs = grad_one + grad_input_in
    output, grad_tokens = regroup(
        (final.astype(jnp.bfloat16), grad_inputs.astype(jnp.bfloat16)),
        back_select,
        back_place,
        groups,
    )
    grad_passages = grad_memory_rows.astype(jnp.bfloat16).reshape(passages.shape)
    summed = (
        lax.psum(triple_grad.astype(jnp.bfloat16), "dp").astype(jnp.float32),
        lax.psum(self_out_grad.astype(jnp.bfloat16), "dp").astype(jnp.float32),
        lax.psum(query_grad.astype(jnp.bfloat16), "dp").astype(jnp.float32),
        lax.psum(memory_grad.astype(jnp.bfloat16), "dp").astype(jnp.float32),
        lax.psum(cross_out_grad.astype(jnp.bfloat16), "dp").astype(jnp.float32),
        lax.psum(expand_grad.astype(jnp.bfloat16), "dp").astype(jnp.float32),
        lax.psum(contract_grad.astype(jnp.bfloat16), "dp").astype(jnp.float32),
    )
    norm_grads = lax.psum(
        (jnp.stack([gain_one, gain_two, gain_three]), jnp.stack([bias_one, bias_two, bias_three])),
        ("dp", "row"),
    )
    return (
        output,
        grad_tokens,
        grad_passages,
        summed[0],
        summed[1],
        summed[2],
        summed[3],
        summed[4],
        summed[5],
        summed[6],
        norm_grads[0],
        norm_grads[1],
    )


def solution(mesh):
    in_specs = (
        P(("dp", "row"), "col"),
        P(("dp", "row"), None, "col"),
        P(),
        P(),
        P(),
        P("col", None, "row"),
        P("row", "col"),
        P("col", None, "row"),
        P("col", None, "row"),
        P("row", "col"),
        P("col", None, "row"),
        P("row", "col"),
        P(None, "col"),
        P(None, "col"),
        P(("dp", "row"), "col"),
    )
    out_specs = (
        P(("dp", "row"), "col"),
        P(("dp", "row"), "col"),
        P(("dp", "row"), None, "col"),
        P("col", None, "row"),
        P("row", "col"),
        P("col", None, "row"),
        P("col", None, "row"),
        P("row", "col"),
        P("col", None, "row"),
        P("row", "col"),
        P(None, "col"),
        P(None, "col"),
    )
    return jax.shard_map(
        on_device, mesh=mesh, in_specs=in_specs, out_specs=out_specs, check_vma=False
    )
```

profile of v0, /device:TPU:0, one launch (start us, length us, event | category | flops | bytes accessed | tf_op | source)
XLA Modules:
  0.0 2578.9 jit_solution(11283841143695889558)
XLA Ops:
  33.0 22.4 all-gather.16.cloned.1.call-done
  63.7 211.3 %reduce-scatter.19.cloned.1.call-done = f32[2048,3,128]{2,0,1:T(8,128)} async-done(((f32[2048,3,512]{2,0,1:T(8,128)}), f32[2048,3,128]{2,0,1:T(8,128)}) %reduce-scatter.19.cloned.1.call-update) | async-done | bytes 3145744 | tf_op jit(solution)/shard_map/reduce_scatter | solution.py:54
  280.2 39.3 %while.54 = (s32[]{:T(128)}, bf16[4,512,2,64]{1,3,2,0:T(8,128)(2,1)S(1)}, f32[4,2,512]{2,1,0:T(2,128)S(1)}, s32[4]{0:T(128)S(1)}, s32[]{:T(128)S(1)}, /*index=5*...) while((s32[]{:T(128)}, ...), condition=%wide.region_8.9_spmd, body=%wide.region_5.8_spmd.sunk | while | flops 565248512 | bytes 30712012 | solution.py:144
  320.9 46.8 %all-gather.18.cloned.1.call-done = bf16[2048,512]{0,1:T(8,128)(2,1)} async-done(((bf16[2048,128]{0,1:T(8,128)(2,1)}), bf16[2048,512]{0,1:T(8,128)(2,1)}) %all-gather.18.cloned.1.call-update) | async-done | bytes 2097168 | tf_op jit(solution)/shard_map/all_gather | solution.py:77
  374.9 27.4 %reduce-scatter.21.cloned.1.call-done = f32[1024,256]{1,0:T(8,128)} async-done(((f32[2048,256]{1,0:T(8,128)}), f32[1024,256]{1,0:T(8,128)}) %reduce-scatter.21.cloned.1.call-update) | async-done | bytes 1048592 | tf_op jit(solution)/shard_map/reduce_scatter | solution.py:82
  455.9 164.9 %reduce-scatter.25.cloned.1.call-done = f32[2400,2,128]{2,0,1:T(8,128)} async-done(((f32[2400,2,512]{2,0,1:T(8,128)}), f32[2400,2,128]{2,0,1:T(8,128)}) %reduce-scatter.25.cloned.1.call-update) | async-done | bytes 2457616 | tf_op jit(solution)/shard_map/reduce_scatter | solution.py:54
  627.4 73.5 %reduce-scatter.23.cloned.1.call-done = f32[2048,1,128]{2,0,1:T(8,128)} async-done(((f32[2048,1,512]{2,0,1:T(8,128)}), f32[2048,1,128]{2,0,1:T(8,128)}) %reduce-scatter.23.cloned.1.call-update) | async-done | bytes 1048592 | tf_op jit(solution)/shard_map/reduce_scatter | solution.py:54
  706.5 51.5 %while.55 = (s32[]{:T(128)}, bf16[4,512,2,64]{1,3,2,0:T(8,128)(2,1)}, f32[4,2,512]{2,1,0:T(2,128)}, s32[4]{0:T(128)S(1)}, s32[]{:T(128)S(1)}, /*index=5*/pred[2,...) while((s32[]{:T(128)}, ...), condition=%wide.region_20.21_spmd, body=%wide.region_17.20_spmd.sunk | while | flops 659931136 | bytes 35945748 | solution.py:144
  760.5 46.2 %all-gather.24.cloned.1.call-done = bf16[2048,512]{0,1:T(8,128)(2,1)} async-done(((bf16[2048,128]{0,1:T(8,128)(2,1)}), bf16[2048,512]{0,1:T(8,128)(2,1)}) %all-gather.24.cloned.1.call-update) | async-done | bytes 2097168 | tf_op jit(solution)/shard_map/all_gather | solution.py:77
  810.5 30.8 %reduce-scatter.27.cloned.1.call-done = f32[1024,256]{1,0:T(8,128)} async-done(((f32[2048,256]{1,0:T(8,128)}), f32[1024,256]{1,0:T(8,128)}) %reduce-scatter.27.cloned.1.call-update) | async-done | bytes 1048592 | tf_op jit(solution)/shard_map/reduce_scatter | solution.py:82
  886.6 280.6 %reduce-scatter.29.cloned.1.call-done = f32[2048,1,512]{2,0,1:T(8,128)} async-done(((f32[2048,1,2048]{2,0,1:T(8,128)}), f32[2048,1,512]{2,0,1:T(8,128)}) %reduce-scatter.29.cloned.1.call-update) | async-done | bytes 4194320 | tf_op jit(solution)/shard_map/reduce_scatter | solution.py:54
  1178.7 150.3 %all-gather.28.cloned.1.call-done = bf16[2048,2048]{1,0:T(8,128)(2,1)} async-done(((bf16[2048,512]{1,0:T(8,128)(2,1)}), bf16[2048,2048]{1,0:T(8,128)(2,1)}) %all-gather.28.cloned.1.call-update) | async-done | bytes 8388624 | tf_op jit(solution)/shard_map/all_gather | solution.py:77
  1395.0 19.9 all-gather.30.cloned.1.call-done
  1421.9 144.7 %reduce-scatter.33.cloned.1.call-done = bf16[2048,512]{1,0:T(8,128)(2,1)} async-done(((bf16[2048,2048]{1,0:T(8,128)(2,1)}), bf16[2048,512]{1,0:T(8,128)(2,1)}) %reduce-scatter.33.cloned.1.call-update) | async-done | bytes 2097168 | tf_op jit(solution)/shard_map/reduce_scatter | solution.py:95
  1572.6 150.3 %all-gather.42.cloned.1.call-done = bf16[2048,2048]{1,0:T(8,128)(2,1)} async-done(((bf16[2048,512]{1,0:T(8,128)(2,1)}), bf16[2048,2048]{1,0:T(8,128)(2,1)}) %all-gather.42.cloned.1.call-update) | async-done | bytes 8388624 | tf_op jit(solution)/shard_map/all_gather | solution.py:59
  1792.0 43.3 %reduce-scatter.43.cloned.1.call-done = bf16[128,2048]{1,0:T(8,128)(2,1)} async-done(((bf16[512,2048]{1,0:T(8,128)(2,1)}), bf16[128,2048]{1,0:T(8,128)(2,1)}) %reduce-scatter.43.cloned.1.call-update) | async-done | bytes 524304
  1836.7 140.2 %while.56 = (s32[]{:T(128)}, f32[2400,2,64]{0,2,1:T(8,128)}, f32[2400,2,64]{0,2,1:T(8,128)S(1)}, bf16[4,512,2,64]{1,3,2,0:T(8,128)(2,1)}, s32[4]{0:T(128)}, /*in...) while((s32[]{:T(128)}, f32[2400,2,64]{0,2,1:T(8,128)}, ...), condition=%wide.region_46.47_spmd.clone, body=%wide.region_44.46_spmd.clone.sunk | while | flops 1597812736 | bytes 158928496 | solution.py:183
  1980.0 45.0 %all-gather.34.cloned.1.call-done = bf16[2048,1,512]{0,2,1:T(8,128)(2,1)} async-done(((bf16[2048,1,128]{0,2,1:T(8,128)(2,1)}), bf16[2048,1,512]{0,2,1:T(8,128)(2,1)}) %all-gather.34.cloned.1.call-update) | async-done | bytes 2097168 | tf_op jit(solution)/shard_map/all_gather | solution.py:59
  2028.4 19.3 reduce-scatter.37.cloned.1.call-done
  2088.4 43.7 %reduce-scatter.45.cloned.1.call-done = bf16[128,2048]{1,0:T(8,128)(2,1)} async-done(((bf16[512,2048]{1,0:T(8,128)(2,1)}), bf16[128,2048]{1,0:T(8,128)(2,1)}) %reduce-scatter.45.cloned.1.call-update) | async-done | bytes 524304
  2132.2 68.6 %while.57 = (s32[]{:T(128)}, f32[2048,2,64]{0,2,1:T(8,128)S(1)}, f32[2048,2,64]{0,2,1:T(8,128)}, bf16[4,512,2,64]{1,3,2,0:T(8,128)(2,1)S(1)}, s32[4]{0:T(128)S(1...) while((s32[]{:T(128)}, f32[2048,2,64]{0,2,1:T(8,128)S(1)}, ...), condition=%wide.region_55.56_spmd.clone, body=%wide.region_53.55_spmd.clone.sunk | while | flops 1378157056 | bytes 84185424 | solution.py:183
  2211.1 112.1 %all-gather.38.cloned.1.call-done = bf16[2048,3,512]{2,0,1:T(8,128)(2,1)} async-done(((bf16[2048,3,128]{2,0,1:T(8,128)(2,1)}), bf16[2048,3,512]{2,0,1:T(8,128)(2,1)}) %all-gather.38.cloned.1.call-update) | async-done | bytes 6291472 | tf_op jit(solution)/shard_map/all_gather | solution.py:59
  2336.7 79.0 %all-gather.40.cloned.1.call-done = bf16[2400,2,512]{2,0,1:T(8,128)(2,1)} async-done(((bf16[2400,2,128]{2,0,1:T(8,128)(2,1)}), bf16[2400,2,512]{2,0,1:T(8,128)(2,1)}) %all-gather.40.cloned.1.call-update) | async-done | bytes 4915216 | tf_op jit(solution)/shard_map/all_gather | solution.py:59
  2483.2 71.2 %all-reduce.10.cloned.1.call-done = (bf16[256,1,512]{2,0,1:T(8,128)(2,1)}, bf16[256,2,512]{0,2,1:T(8,128)(2,1)}, bf16[256,1,2048]{2,0,1:T(8,128)(2,1)}, bf16[256...) async-done(((bf16[256,1,512]{2,0,1:T(8,128)(2,1)}, bf16[256,2,512]{0,2,1:T(8,128)(2,1)}, ...) | async-done | bytes 4194320 | tf_op jit(solution)/shard_map/psum | solution.py:331
  (598 shorter events, 768.8 us)
Async XLA Ops:
  32.9 242.1 %reduce-scatter.19.cloned.1.call-start = ((), (), s32[]{:S(2)}) async-start(), calls=%async_computation.19 | async-start | bytes 15728640 | tf_op jit(solution)/shard_map/reduce_scatter | solution.py:54
  63.0 304.8 %all-gather.18.cloned.1.call-start = ((), (), s32[]{:S(2)}) async-start(), calls=%async_computation.20 | async-start | bytes 2621440 | tf_op jit(solution)/shard_map/all_gather | solution.py:77
  320.9 81.5 %reduce-scatter.21.cloned.1.call-start = ((), (), s32[]{:S(2)}) async-start(), calls=%async_computation.21 | async-start | bytes 3145728 | tf_op jit(solution)/shard_map/reduce_scatter | solution.py:82
  373.7 77.2 %all-gather.20.cloned.1.call-start = ((), (), s32[]{:S(2)}) async-start(), calls=%async_computation.22 | async-start | bytes 1572864 | tf_op jit(solution)/shard_map/all_gather | solution.py:52
  417.1 203.7 %reduce-scatter.25.cloned.1.call-start = ((), (), s32[]{:S(2)}) async-start(), calls=%async_computation.25 | async-start | bytes 12288000 | tf_op jit(solution)/shard_map/reduce_scatter | solution.py:54
  434.4 266.6 %reduce-scatter.23.cloned.1.call-start = ((), (), s32[]{:S(2)}) async-start(), calls=%async_computation.23 | async-start | bytes 5242880 | tf_op jit(solution)/shard_map/reduce_scatter | solution.py:54
  455.0 351.8 %all-gather.24.cloned.1.call-start = ((), (), s32[]{:S(2)}) async-start(), calls=%async_computation.26 | async-start | bytes 2621440 | tf_op jit(solution)/shard_map/all_gather | solution.py:77
  760.5 80.8 %reduce-scatter.27.cloned.1.call-start = ((), (), s32[]{:S(2)}) async-start(), calls=%async_computation.27 | async-start | bytes 3145728 | tf_op jit(solution)/shard_map/reduce_scatter | solution.py:82
  858.2 308.9 %reduce-scatter.29.cloned.1.call-start = ((), (), s32[]{:S(2)}) async-start(), calls=%async_computation.29 | async-start | bytes 20971520 | tf_op jit(solution)/shard_map/reduce_scatter | solution.py:54
  886.6 442.4 %all-gather.28.cloned.1.call-start = ((), (), s32[]{:S(2)}) async-start(), calls=%async_computation.30 | async-start | bytes 10485760 | tf_op jit(solution)/shard_map/all_gather | solution.py:77
  1178.6 187.7 %reduce-scatter.31.cloned.1.call-start = ((), (), s32[]{:S(2)}) async-start(), calls=%async_computation.31 | async-start | bytes 3145728 | tf_op jit(solution)/shard_map/reduce_scatter | solution.py:82
  1336.1 78.8 %all-gather.30.cloned.1.call-start = ((), (), s32[]{:S(2)}) async-start(), calls=%async_computation.32 | async-start | bytes 1572864 | tf_op jit(solution)/shard_map/all_gather | solution.py:92
  1394.8 171.8 %reduce-scatter.33.cloned.1.call-start = ((), (), s32[]{:S(2)}) async-start(), calls=%async_computation.33 | async-start | bytes 10485760 | tf_op jit(solution)/shard_map/reduce_scatter | solution.py:95
  1421.8 301.1 %all-gather.42.cloned.1.call-start = ((), (), s32[]{:S(2)}) async-start(), calls=%async_computation.43 | async-start | bytes 10485760 | tf_op jit(solution)/shard_map/all_gather | solution.py:59
  1572.6 176.1 %reduce-scatter.35.cloned.1.call-start = ((), (), s32[]{:S(2)}) async-start(), calls=%async_computation.34 | async-start | bytes 1572864 | tf_op jit(solution)/shard_map/reduce_scatter | solution.py:65
  1765.6 69.8 %reduce-scatter.43.cloned.1.call-start = ((), (), s32[]{:S(2)}) async-start(), calls=%async_computation.44 | async-start | bytes 2621440
  1791.6 233.4 %all-gather.34.cloned.1.call-start = ((), (), s32[]{:S(2)}) async-start(), calls=%async_computation.36 | async-start | bytes 2621440 | tf_op jit(solution)/shard_map/all_gather | solution.py:59
  1980.0 67.7 %reduce-scatter.37.cloned.1.call-start = ((), (), s32[]{:S(2)}) async-start(), calls=%async_computation.37 | async-start | bytes 1572864 | tf_op jit(solution)/shard_map/reduce_scatter | solution.py:65
  2088.4 234.8 %all-gather.38.cloned.1.call-start = ((), (), s32[]{:S(2)}) async-start(), calls=%async_computation.39 | async-start | bytes 7864320 | tf_op jit(solution)/shard_map/all_gather | solution.py:59
  2209.0 206.7 %all-gather.40.cloned.1.call-start = ((), (), s32[]{:S(2)}) async-start(), calls=%async_computation.41 | async-start | bytes 6144000 | tf_op jit(solution)/shard_map/all_gather | solution.py:59
  2211.1 234.7 %reduce-scatter.39.cloned.1.call-start = ((), (), s32[]{:S(2)}) async-start(), calls=%async_computation.40 | async-start | bytes 1572864 | tf_op jit(solution)/shard_map/reduce_scatter | solution.py:65
  2329.0 151.9 %reduce-scatter.41.cloned.1.call-start = ((), (), s32[]{:S(2)}) async-start(), calls=%async_computation.42 | async-start | bytes 1843200 | tf_op jit(solution)/shard_map/reduce_scatter | solution.py:65
  2420.7 133.8 %all-reduce.10.cloned.1.call-start = ((), (), s32[]{:S(2)}) async-start(), calls=%async_computation.46 | async-start | bytes 8388608 | tf_op jit(solution)/shard_map/psum | solution.py:331
  2460.1 110.4 %all-to-all-start.3 = ((bf16[4,512,256]{2,1,0:T(8,128)(2,1)}), bf16[4,512,256]{2,1,0:T(8,128)(2,1)S(1)}, u32[]{:S(2)}, u32[]{:S(2)}) async-start(bf16[4,512,256]{2,1,0:T(8,128)(2,1)} %bitcast.62), calls=%async_computation.14 | async-start | bytes 2097152 | tf_op jit(solution)/shard_map/all_to_all | solution.py:46
  (127 other events, 5364.5 us)
Sparse Core Ops, SparseCore 0:
  33.1 22.2 all-gather.15
  63.1 211.8 reduce-scatter.18
  321.0 46.7 all-gather.17
  371.6 30.6 reduce-scatter.20
  404.3 23.3 all-gather.21
  429.6 21.2 all-gather.19
  453.3 167.4 reduce-scatter.24
  623.1 77.8 reduce-scatter.22
  760.6 46.1 all-gather.23
  810.6 30.6 reduce-scatter.26
  886.7 280.4 reduce-scatter.28
  1178.8 150.2 all-gather.27
  1336.2 30.0 reduce-scatter.30
  1394.9 19.9 all-gather.29
  1421.9 144.6 reduce-scatter.32
  1572.7 150.2 all-gather.41
  1791.7 43.6 reduce-scatter.42
  1980.1 44.8 all-gather.33
  2028.5 19.1 reduce-scatter.36
  2088.5 43.6 reduce-scatter.44
  2209.1 113.9 all-gather.37
  2325.2 90.4 all-gather.39
  2439.8 22.3 reduce-scatter.40
  2466.3 88.1 all-reduce.9
  (5 shorter events, 92.3 us)
where the time goes:
time: 2590 us; the launch traced here: 2580 us
  waiting for transfers between devices  1910 us (74%)
  matrix products  253 us (10%)
  other arithmetic  172 us (7%)
  blocking collectives  103 us (4%)
  local copies, waits for them, and re-layouts  96.8 us (4%)
    reduce_scatter x4, waiting for transfers between devices, project_in(): lax.psum_scatter(partial_sum, 'col', scatter_dimension=2, tiled=True)  730 us
    all_gather x4, waiting for transfers between devices, project_in_back(): wide = lax.all_gather(grad_low, 'col', axis=2, tiled=True)  386 us
    all_gather x3, waiting for transfers between devices, project_out(): wide = lax.all_gather(heads_low, 'col', axis=1, tiled=True)  243 us
    reduce_scatter x1, waiting for transfers between devices, project_out_back(): lax.psum_scatter(partial_sum.astype(jnp.bfloat16), 'col', scatter_dimensi...  145 us
    unnamed x31, waiting for transfers between devices  87.5 us
    psum x1, waiting for transfers between devices, on_device(): lax.psum(query_grad.astype(jnp.bfloat16), 'dp').astype(jnp.float32)  71.2 us
    psum x6, blocking collectives, row_sums(): return lax.psum((jnp.sum(first_terms, 1), jnp.sum(second_terms, 1)), 'col')  68.2 us
    all_gather x4, waiting for transfers between devices, project_in(): gathered = lax.all_gather(rows_low, 'row', axis=0, tiled=True)  67.5 us
  transfers between devices with their start and end apart: 32, of which 29 were waited for; matrix products, arithmetic and copies ran while one was open for 4% of the time, Pallas kernels for 0%

commit v1 on v0

v1 whole, which is shorter than its diff:
```python
import jax
import jax.numpy as jnp
from jax import lax
from jax.experimental import pallas as pl
from jax.experimental.pallas import tpu as pltpu
from jax.sharding import PartitionSpec as P

HD = 64
PAIR = 2 * HD
PLEN = 300
TOPP = 5
PP_GRP = 8
BLK = 128
SPAN = 304


epsilon = 1e-05
LOW = -1e30
FACTOR = HD ** (-0.5)


def swap_row(value):
    return lax.ppermute(value, "row", [(0, 1), (1, 0)])


def to_tokens(rows):
    cols = lax.axis_size("col")
    count, width = rows.shape
    got = lax.all_to_all(rows.reshape(cols, count // cols, width), "col", 0, 0, tiled=True)
    return got.transpose(1, 0, 2).reshape(count // cols, cols * width)


def to_features(rows):
    cols = lax.axis_size("col")
    count, width = rows.shape
    parts = rows.reshape(count, cols, width // cols).transpose(1, 0, 2)
    return lax.all_to_all(parts, "col", 0, 0, tiled=True).reshape(count * cols, width // cols)


def to_heads(rows):
    return to_features(rows)


def from_heads(rows):
    return to_tokens(rows)


def regroup(value, select, placing, groups):
    width = value.shape[-1]
    out = value.reshape(-1, BLK, width)[select]
    moved = lax.all_to_all(out, "dp", split_axis=0, concat_axis=0, tiled=True)
    return moved[placing].reshape(-1, width)


def gather_in(weight):
    return lax.all_gather(weight, "col", axis=0, tiled=True)


def gather_out(weight):
    return lax.all_gather(weight, "col", axis=0, tiled=False)


def dot(left, right):
    return jnp.dot(left, right, preferred_element_type=jnp.float32)


def in_proj(rows, weight):
    return jnp.einsum("tf,fe->te", rows, weight, preferred_element_type=jnp.float32)


def in_proj_back(grad, weight):
    return jnp.einsum("te,fe->tf", grad, weight, preferred_element_type=jnp.float32)


def out_proj(rows, weight):
    out = jnp.einsum("te,cef->tcf", rows, weight, preferred_element_type=jnp.float32)
    return out.reshape(rows.shape[0], -1)


def out_proj_back(grad, weight):
    parts = grad.reshape(grad.shape[0], weight.shape[0], weight.shape[2])
    return jnp.einsum("tcf,cef->te", parts, weight, preferred_element_type=jnp.float32)


def in_weight_grad(rows, grad):
    return jnp.einsum("tf,te->fe", rows, grad, preferred_element_type=jnp.float32).astype(
        jnp.bfloat16
    )


def out_weight_grad(rows, grad, cols):
    parts = grad.reshape(grad.shape[0], cols, -1)
    return jnp.einsum("te,tcf->cef", rows, parts, preferred_element_type=jnp.float32).astype(
        jnp.bfloat16
    )


def reduce_weight(grad):
    cols = lax.axis_size("col")
    flat = grad.reshape(-1, grad.shape[-1])
    part = lax.psum_scatter(flat, ("col", "dp"), scatter_dimension=0, tiled=True)
    return lax.all_gather(part, "dp", axis=0, tiled=True).astype(jnp.float32)


def both_halves(part):
    own = part.shape[0] // 2
    low = part.astype(jnp.bfloat16)
    upper = part[:own] + swap_row(low[own:]).astype(jnp.float32)
    lower = part[own:] + swap_row(low[:own]).astype(jnp.float32)
    return jnp.concatenate([upper, lower], 0)


def norm_forward(value, gain, offset):
    center = jnp.mean(value, 1, keepdims=True)
    moved = value - center
    scale = lax.rsqrt(jnp.mean(moved * moved, 1, keepdims=True) + epsilon)
    normed = moved * scale
    return (normed * gain + offset, normed, scale)


def norm_back(grad, normed, scale, gain):
    scaled = grad * gain
    total = jnp.mean(scaled, 1, keepdims=True)
    crossed = jnp.mean(scaled * normed, 1, keepdims=True)
    return scale * (scaled - total - normed * crossed)


def norm_param_sums(grad, normed, own):
    return (jnp.sum(grad[:own] * normed[:own], 0), jnp.sum(grad[:own], 0))


def nt(left, right):
    return lax.dot_general(
        left, right, (((1,), (1,)), ((), ())), preferred_element_type=jnp.float32
    )


def nn(left, right):
    return jnp.dot(left, right, preferred_element_type=jnp.float32)


def flip(value):
    return value.astype(jnp.float32).T.astype(jnp.bfloat16)


def stack_heads(value):
    lane = lax.broadcasted_iota(jnp.int32, value.shape, 1) // HD
    wide = value.astype(jnp.float32)
    parts = [jnp.where(lane == h, wide, 0.0) for h in range(2)]
    return jnp.concatenate(parts, 0).astype(jnp.bfloat16)


def fresh_state(count):
    return (
        jnp.full((1, count), LOW, jnp.float32),
        jnp.zeros((1, count), jnp.float32),
        jnp.zeros((HD, count), jnp.float32),
    )


def per_head(flipped, wide):
    count = wide.shape[1] // 2
    return jnp.concatenate(
        [nn(flipped[h * HD : (h + 1) * HD], wide[:, h * count : (h + 1) * count]) for h in range(2)],
        1,
    )


def step_forward(state, scores, v_flipped):
    top, total, out = state
    fresh = jnp.maximum(top, jnp.max(scores, 0, keepdims=True))
    keep = jnp.exp(top - fresh)
    expo = jnp.exp(scores - fresh)
    total = total * keep + jnp.sum(expo, 0, keepdims=True)
    out = out * keep + per_head(v_flipped, expo.astype(jnp.bfloat16))
    return (fresh, total, out)


def rows_of(out):
    count = out.shape[1] // 2
    return jnp.concatenate([out[:, :count], out[:, count:]], 0).T


def finish_forward(state, o_ref, lse_ref):
    top, total, out = state
    o_ref[...] = rows_of(out / total).astype(jnp.bfloat16)
    lse_ref[...] = (top + jnp.log(total)).reshape(lse_ref.shape)


def delta_of(out, up):
    both = (out.astype(jnp.float32) * up.astype(jnp.float32)).T
    return jnp.concatenate(
        [jnp.sum(both[h * HD : (h + 1) * HD], 0, keepdims=True) for h in range(2)], 1
    )


def step_backward(scores, lse, delta, value, up, queries, k_flipped):
    probs = jnp.exp(scores - lse)
    grad_value = nn(probs.astype(jnp.bfloat16), up)
    grad_scores = (probs * (nt(value, up) - delta)).astype(jnp.bfloat16)
    return grad_value, nn(grad_scores, queries), per_head(k_flipped, grad_scores)


def self_spans(i, first, tile):
    start = i * tile
    begin = jnp.where(start >= first, first, 0)
    begin_last = jnp.where(start + tile - 1 >= first, first, 0)
    low = begin // tile
    middle = jnp.minimum((begin_last + tile - 1) // tile, i)
    return low, jnp.maximum(middle, low)


def self_masked(scores, i, j, first, tile):
    count = scores.shape[1]
    key_pos = j * tile + lax.broadcasted_iota(jnp.int32, scores.shape, 0)
    lane = lax.broadcasted_iota(jnp.int32, (1, count), 1)
    query_pos = i * tile + jnp.where(lane >= tile, lane - tile, lane)
    begin = jnp.where(query_pos >= first, first, 0)
    return jnp.where((key_pos <= query_pos) & (key_pos >= begin), scores, LOW)


def self_forward_kernel(tiles, tile, info, q_ref, k_ref, v_ref, o_ref, lse_ref, v_flipped):
    i = pl.program_id(0)
    first = info[tiles]

    @pl.when(i == 0)
    def _():
        for j in range(tiles):
            v_flipped[j] = flip(v_ref[j * tile : (j + 1) * tile, :])

    queries = stack_heads(q_ref[...].astype(jnp.float32) * FACTOR)
    low, middle = self_spans(i, first, tile)

    def visit(masked):
        def body(j, state):
            at = info[j]
            keys = k_ref[pl.ds(pl.multiple_of(at * tile, tile), tile), :]
            scores = nt(keys, queries)
            if masked:
                scores = self_masked(scores, i, j, first, tile)
            return step_forward(state, scores, v_flipped[at])

        return body

    state = fresh_state(2 * tile)
    state = lax.fori_loop(low, middle, visit(True), state)
    state = lax.fori_loop(middle, i, visit(False), state)
    finish_forward(visit(True)(i, state), o_ref, lse_ref)


def self_backward_kernel(
    tiles, tile, info, q_ref, k_ref, v_ref, o_ref, up_ref, lse_ref,
    dq_ref, dk_ref, dv_ref, k_flipped, dk_sum, dv_sum,
):
    i = pl.program_id(0)
    first = info[tiles]

    @pl.when(i == 0)
    def _():
        for j in range(tiles):
            k_flipped[j] = flip(k_ref[j * tile : (j + 1) * tile, :])
        dk_sum[...] = jnp.zeros_like(dk_sum)
        dv_sum[...] = jnp.zeros_like(dv_sum)

    queries = stack_heads(q_ref[...].astype(jnp.float32) * FACTOR)
    up = stack_heads(up_ref[...])
    delta = delta_of(o_ref[...], up_ref[...])
    lse = lse_ref[...].reshape(1, 2 * tile)
    low, middle = self_spans(i, first, tile)

    def visit(masked):
        def body(j, total):
            at = info[j]
            rows = pl.ds(pl.multiple_of(at * tile, tile), tile)
            scores = nt(k_ref[rows, :], queries)
            if masked:
                scores = self_masked(scores, i, j, first, tile)
            gv, gk, gq = step_backward(
                scores, lse, delta, v_ref[rows, :], up, queries, k_flipped[at]
            )
            dv_sum[rows, :] += gv
            dk_sum[rows, :] += gk
            return total + gq

        return body

    total = jnp.zeros((HD, 2 * tile), jnp.float32)
    total = lax.fori_loop(low, middle, visit(True), total)
    total = lax.fori_loop(middle, i, visit(False), total)
    total = visit(True)(i, total)
    dq_ref[...] = (rows_of(total) * FACTOR).astype(jnp.bfloat16)

    @pl.when(i == tiles - 1)
    def _():
        dk_ref[...] = dk_sum[...].astype(jnp.bfloat16)
        dv_ref[...] = dv_sum[...].astype(jnp.bfloat16)


def cost(flops, elements, size):
    return pl.CostEstimate(flops=flops, bytes_accessed=size, transcendentals=elements)


def self_attend(q, k, v, info, tile):
    total = q.shape[0]
    tiles = total // tile
    part = pl.BlockSpec((tile, PAIR), lambda i, info: (info[i], 0))
    whole = pl.BlockSpec((total, PAIR), lambda i, info: (0, 0))
    stat = pl.BlockSpec((1, 1, 2 * tile), lambda i, info: (i, 0, 0))
    elements = total * total
    return pl.pallas_call(
        lambda *refs: self_forward_kernel(tiles, tile, *refs),
        out_shape=(
            jax.ShapeDtypeStruct((total, PAIR), jnp.bfloat16),
            jax.ShapeDtypeStruct((tiles, 1, 2 * tile), jnp.float32),
        ),
        grid_spec=pltpu.PrefetchScalarGridSpec(
            num_scalar_prefetch=1,
            grid=(tiles,),
            in_specs=[part, whole, whole],
            out_specs=(part, stat),
            scratch_shapes=[pltpu.VMEM((tiles, PAIR, tile), jnp.bfloat16)],
        ),
        cost_estimate=cost(8 * elements * PAIR, elements, 4 * total * PAIR * 2),
        name="self_attend",
    )(info, q, k, v)


def self_attend_back(q, k, v, out, up, lse, info, tile):
    total = q.shape[0]
    tiles = total // tile
    part = pl.BlockSpec((tile, PAIR), lambda i, info: (info[i], 0))
    whole = pl.BlockSpec((total, PAIR), lambda i, info: (0, 0))
    stat = pl.BlockSpec((1, 1, 2 * tile), lambda i, info: (i, 0, 0))
    elements = total * total
    like = jax.ShapeDtypeStruct((total, PAIR), jnp.bfloat16)
    return pl.pallas_call(
        lambda *refs: self_backward_kernel(tiles, tile, *refs),
        out_shape=(like, like, like),
        grid_spec=pltpu.PrefetchScalarGridSpec(
            num_scalar_prefetch=1,
            grid=(tiles,),
            in_specs=[part, whole, whole, part, part, stat],
            out_specs=(part, whole, whole),
            scratch_shapes=[
                pltpu.VMEM((tiles, PAIR, tile), jnp.bfloat16),
                pltpu.VMEM((total, PAIR), jnp.float32),
                pltpu.VMEM((total, PAIR), jnp.float32),
            ],
        ),
        cost_estimate=cost(20 * elements * PAIR, elements, 8 * total * PAIR * 2),
        name="self_attend_back",
    )(info, q, k, v, out, up, lse)


def cross_scores(keys, queries, bias, valid):
    scores = nt(keys, queries) + bias
    tail = scores.shape[0] - 8
    row = lax.broadcasted_iota(jnp.int32, (8, scores.shape[1]), 0)
    return jnp.concatenate(
        [scores[:tail], jnp.where(row < valid - tail, scores[tail:], LOW)], 0
    )


def cross_bias(info, side, passages, at, count):
    base = side * (passages + 2)
    switch = info[base + passages + 1]
    flags = info[2 * (passages + 2) + at]
    lane = lax.broadcasted_iota(jnp.int32, (1, 2 * count), 1)
    place = jnp.where(lane >= count, lane - count, lane)
    reads = jnp.where(place < switch, flags & 1, flags >> 1)
    return jnp.where(reads > 0, 0.0, LOW)


def cross_forward_kernel(passages, span, valid, info, q_ref, k_ref, v_ref, o_ref, lse_ref, v_flipped):
    side = pl.program_id(1)
    count = q_ref.shape[0]

    @pl.when(side == 0)
    def _():
        for j in range(passages):
            v_flipped[j] = flip(v_ref[j * span : (j + 1) * span, :])

    queries = stack_heads(q_ref[...].astype(jnp.float32) * FACTOR)
    base = side * (passages + 2)

    def body(t, state):
        at = info[base + t]
        keys = k_ref[pl.ds(pl.multiple_of(at * span, 16), span), :]
        scores = cross_scores(keys, queries, cross_bias(info, side, passages, at, count), valid)
        return step_forward(state, scores, v_flipped[at])

    state = lax.fori_loop(0, info[base + passages], body, fresh_state(2 * count))
    finish_forward(state, o_ref, lse_ref)


def cross_backward_kernel(
    passages, span, valid, info, q_ref, k_ref, v_ref, o_ref, up_ref, lse_ref,
    dq_ref, dkv_ref, k_flipped, dk_sum, dv_sum,
):
    pair = pl.program_id(0)
    side = pl.program_id(1)
    count = q_ref.shape[0]

    @pl.when(side == 0)
    def _():
        for j in range(passages):
            k_flipped[j] = flip(k_ref[j * span : (j + 1) * span, :])
        dk_sum[...] = jnp.zeros_like(dk_sum)
        dv_sum[...] = jnp.zeros_like(dv_sum)

    queries = stack_heads(q_ref[...].astype(jnp.float32) * FACTOR)
    up = stack_heads(up_ref[...])
    delta = delta_of(o_ref[...], up_ref[...])
    lse = lse_ref[...].reshape(1, 2 * count)
    base = side * (passages + 2)

    def body(t, total):
        at = info[base + t]
        rows = pl.ds(pl.multiple_of(at * span, 16), span)
        scores = cross_scores(
            k_ref[rows, :], queries, cross_bias(info, side, passages, at, count), valid
        )
        gv, gk, gq = step_backward(scores, lse, delta, v_ref[rows, :], up, queries, k_flipped[at])
        dv_sum[rows, :] += gv
        dk_sum[rows, :] += gk
        return total + gq

    total = jnp.zeros((HD, 2 * count), jnp.float32)
    total = lax.fori_loop(0, info[base + passages], body, total)
    dq_ref[...] = (rows_of(total) * FACTOR).astype(jnp.bfloat16)

    @pl.when(side == 1)
    def _():
        pairs = pl.num_programs(0)
        width = dkv_ref.shape[1] // 2
        dkv_ref[:, pl.ds(pl.multiple_of(pair * PAIR, PAIR), PAIR)] = dk_sum[...].astype(jnp.bfloat16)
        dkv_ref[:, pl.ds(pl.multiple_of(width + pair * PAIR, PAIR), PAIR)] = dv_sum[...].astype(
            jnp.bfloat16
        )


def cross_attend(q, kv, info, passages, valid):
    rows, width = q.shape
    keys = kv.shape[0]
    pairs = width // PAIR
    count = rows // 2
    span = keys // passages
    part = pl.BlockSpec((count, PAIR), lambda p, s, info: (s, p))
    k_spec = pl.BlockSpec((keys, PAIR), lambda p, s, info: (0, p))
    v_spec = pl.BlockSpec((keys, PAIR), lambda p, s, info: (0, pairs + p))
    stat = pl.BlockSpec((1, 1, 1, 2 * count), lambda p, s, info: (p, s, 0, 0))
    elements = rows * keys * 2 * pairs
    return pl.pallas_call(
        lambda *refs: cross_forward_kernel(passages, span, valid, *refs),
        out_shape=(
            jax.ShapeDtypeStruct((rows, width), jnp.bfloat16),
            jax.ShapeDtypeStruct((pairs, 2, 1, 2 * count), jnp.float32),
        ),
        grid_spec=pltpu.PrefetchScalarGridSpec(
            num_scalar_prefetch=1,
            grid=(pairs, 2),
            in_specs=[part, k_spec, v_spec],
            out_specs=(part, stat),
            scratch_shapes=[pltpu.VMEM((passages, PAIR, span), jnp.bfloat16)],
        ),
        cost_estimate=cost(8 * elements * PAIR, elements, kv.size * 2),
        name="cross_attend",
    )(info, q, kv, kv)


def cross_attend_back(q, kv, out, up, lse, info, passages, valid):
    rows, width = q.shape
    keys = kv.shape[0]
    pairs = width // PAIR
    count = rows // 2
    span = keys // passages
    part = pl.BlockSpec((count, PAIR), lambda p, s, info: (s, p))
    k_spec = pl.BlockSpec((keys, PAIR), lambda p, s, info: (0, p))
    v_spec = pl.BlockSpec((keys, PAIR), lambda p, s, info: (0, pairs + p))
    whole = pl.BlockSpec((keys, 2 * width), lambda p, s, info: (0, 0))
    stat = pl.BlockSpec((1, 1, 1, 2 * count), lambda p, s, info: (p, s, 0, 0))
    elements = rows * keys * 2 * pairs
    return pl.pallas_call(
        lambda *refs: cross_backward_kernel(passages, span, valid, *refs),
        out_shape=(
            jax.ShapeDtypeStruct((rows, width), jnp.bfloat16),
            jax.ShapeDtypeStruct((keys, 2 * width), jnp.bfloat16),
        ),
        grid_spec=pltpu.PrefetchScalarGridSpec(
            num_scalar_prefetch=1,
            grid=(pairs, 2),
            in_specs=[part, k_spec, v_spec, part, part, stat],
            out_specs=(part, whole),
            scratch_shapes=[
                pltpu.VMEM((passages, PAIR, span), jnp.bfloat16),
                pltpu.VMEM((keys, PAIR), jnp.float32),
                pltpu.VMEM((keys, PAIR), jnp.float32),
            ],
        ),
        cost_estimate=cost(20 * elements * PAIR, elements, kv.size * 6),
        name="cross_attend_back",
    )(info, q, kv, kv, out, up, lse)


def gelu_exact(value):
    return jax.nn.gelu(value, approximate=False)


def on_device(
    tokens,
    passages,
    lengths,
    block_order,
    passage_ids,
    triple_weight,
    self_out_weight,
    query_weight,
    memory_weight,
    cross_out_weight,
    expand_weight,
    contract_weight,
    norm_gain,
    norm_bias,
    cotangent,
):
    groups = lax.axis_size("dp")
    row_count = lax.axis_size("row")
    cols = lax.axis_size("col")
    group = lax.axis_index("dp")
    row_index = lax.axis_index("row")
    col_index = lax.axis_index("col")
    own_rows, width = tokens.shape
    features = width * cols
    blocks = own_rows // BLK
    capacity = blocks // (groups // 2)
    span = row_count * blocks
    all_blocks = block_order.shape[0]
    block_ids = jnp.arange(blocks, dtype=jnp.int32)
    slot_ids = jnp.arange(groups * capacity, dtype=jnp.int32)
    inverse = (
        jnp.zeros_like(block_order).at[block_order].set(jnp.arange(all_blocks, dtype=jnp.int32))
    )
    own_blocks = (group * row_count + row_index) * blocks + block_ids
    target = inverse[own_blocks] // span
    earlier = block_ids[None, :] < block_ids[:, None]
    ranking = jnp.sum((target[None, :] == target[:, None]) & earlier, 1)
    matches = (target[None, :] == (slot_ids // capacity)[:, None]) & (
        ranking[None, :] == (slot_ids % capacity)[:, None]
    )
    send_select = jnp.sum(jnp.where(matches, block_ids[None, :], 0), 1)
    back_place = target * capacity + ranking
    wanted = block_order[own_blocks]
    source = wanted // span
    within = wanted % blocks
    rank_in = jnp.sum((source[None, :] == source[:, None]) & (within[None, :] < within[:, None]), 1)
    recv_place = source * capacity + rank_in
    back_matches = recv_place[None, :] == slot_ids[:, None]
    back_select = jnp.sum(jnp.where(back_matches, block_ids[None, :], 0), 1)

    total = own_rows * row_count
    own = own_rows // cols
    first = lax.dynamic_slice_in_dim(lengths, group * 2, 1)[0]
    chosen_ids = lax.dynamic_slice(passage_ids, (group * 2, 0), (2, TOPP)) - group * PP_GRP

    tile_ids = jnp.arange(row_count * cols, dtype=jnp.int32)
    self_info = jnp.concatenate(
        [(tile_ids % cols) * row_count + ((tile_ids // cols) ^ row_index), first[None]]
    )
    pool = passages.shape[0]
    held_passage = ((tile_ids % row_count) ^ row_index) * pool + tile_ids // row_count
    reads = jnp.any(held_passage[None, None, :] == chosen_ids[:, :, None], 1)
    side = jnp.arange(row_count, dtype=jnp.int32)
    switch = jnp.clip(first - (side ^ row_index) * own_rows - col_index * own, 0, own)
    needed = ((switch > 0)[:, None] & reads[0][None]) | ((switch < own)[:, None] & reads[1][None])
    needed = needed.astype(jnp.int32)
    before = jnp.sum(
        needed[:, None, :] * (tile_ids[None, None, :] < tile_ids[None, :, None]), 2
    )
    slots = needed[:, :, None] * (before[:, :, None] == tile_ids[None, None, :])
    listed = jnp.sum(slots * tile_ids[None, :, None], 1)
    per_side = jnp.concatenate([listed, jnp.sum(needed, 1)[:, None], switch[:, None]], 1)
    flags = reads[0].astype(jnp.int32) + 2 * reads[1].astype(jnp.int32)
    cross_info = jnp.concatenate([per_side.reshape(-1), flags]).astype(jnp.int32)
    passage_count = row_count * pool

    def take_tokens(value):
        mine = to_tokens(regroup(value, send_select, recv_place, groups))
        return jnp.concatenate([mine, swap_row(mine)], 0)

    rows_in = take_tokens(tokens)
    upstream = take_tokens(cotangent)
    memory_own = to_tokens(passages.reshape(-1, width))
    memory_own = jnp.pad(memory_own, ((0, SPAN - memory_own.shape[0]), (0, 0)))
    memory = jnp.concatenate([memory_own, swap_row(memory_own)], 0)

    triple_w = gather_in(triple_weight.reshape(width, -1))
    memory_w = gather_in(memory_weight.reshape(width, -1))
    self_out_w = gather_out(self_out_weight)
    query_w = gather_in(query_weight.reshape(width, -1))
    cross_out_w = gather_out(cross_out_weight)
    expand_w = gather_in(expand_weight.reshape(width, -1))
    contract_w = gather_out(contract_weight)
    params = lax.all_gather(jnp.concatenate([norm_gain, norm_bias], 0), "col", axis=1, tiled=True)
    gains = params[:3].astype(jnp.float32)
    offsets = params[3:].astype(jnp.float32)

    feats = rows_in.astype(jnp.float32)
    head_width = triple_weight.shape[2]
    triple = in_proj(rows_in, triple_w).astype(jnp.bfloat16)
    q1, k1, v1 = (
        to_heads(triple[:, i * head_width : (i + 1) * head_width]) for i in range(3)
    )
    attended_heads, self_lse = self_attend(q1, k1, v1, self_info, own)
    attended = from_heads(attended_heads)
    h1, n1, r1 = norm_forward(
        feats + both_halves(out_proj(attended, self_out_w)), gains[0], offsets[0]
    )
    h1b = h1.astype(jnp.bfloat16)
    q2 = in_proj(h1b, query_w).astype(jnp.bfloat16)
    pairs = lax.all_gather(
        in_proj(memory, memory_w).astype(jnp.bfloat16), "col", axis=0, tiled=True
    )
    crossed, cross_lse = cross_attend(q2, pairs, cross_info, passage_count, PLEN)
    h2, n2, r2 = norm_forward(
        h1 + both_halves(out_proj(crossed, cross_out_w)), gains[1], offsets[1]
    )
    h2b = h2.astype(jnp.bfloat16)
    hidden = in_proj(h2b, expand_w)
    active, gelu_pull = jax.vjp(gelu_exact, hidden)
    active = active.astype(jnp.bfloat16)
    final, n3, r3 = norm_forward(
        h2 + both_halves(out_proj(active, contract_w)), gains[2], offsets[2]
    )

    e_out = upstream.astype(jnp.float32)
    e3 = norm_back(e_out, n3, r3, gains[2])
    gain_three, bias_three = norm_param_sums(e_out, n3, own)
    b3 = e3.astype(jnp.bfloat16)
    contract_grad = reduce_weight(out_weight_grad(active, b3, cols))
    grad_hidden = gelu_pull(out_proj_back(b3, contract_w))[0].astype(jnp.bfloat16)
    expand_grad = reduce_weight(in_weight_grad(h2b, grad_hidden))
    up_two = e3 + both_halves(in_proj_back(grad_hidden, expand_w))
    e2 = norm_back(up_two, n2, r2, gains[1])
    gain_two, bias_two = norm_param_sums(up_two, n2, own)
    b2 = e2.astype(jnp.bfloat16)
    cross_out_grad = reduce_weight(out_weight_grad(crossed, b2, cols))
    grad_crossed = out_proj_back(b2, cross_out_w).astype(jnp.bfloat16)
    dq2, grad_pairs = cross_attend_back(
        q2, pairs, crossed, grad_crossed, cross_lse, cross_info, passage_count, PLEN
    )
    grad_pairs = lax.psum_scatter(grad_pairs, "col", scatter_dimension=0, tiled=True)
    query_grad = reduce_weight(in_weight_grad(h1b, dq2))
    up_one = e2 + both_halves(in_proj_back(dq2, query_w))
    e1 = norm_back(up_one, n1, r1, gains[0])
    gain_one, bias_one = norm_param_sums(up_one, n1, own)
    b1 = e1.astype(jnp.bfloat16)
    memory_grad = reduce_weight(in_weight_grad(memory, grad_pairs))
    memory_part = in_proj_back(grad_pairs, memory_w)
    memory_rows = memory_own.shape[0]
    grad_memory = memory_part[:memory_rows] + swap_row(
        memory_part[memory_rows:].astype(jnp.bfloat16)
    ).astype(jnp.float32)
    grad_passages = to_features(grad_memory[:PLEN].astype(jnp.bfloat16)).reshape(passages.shape)

    self_out_grad = reduce_weight(out_weight_grad(attended, b1, cols))
    grad_attended = to_heads(out_proj_back(b1, self_out_w).astype(jnp.bfloat16))
    heads_back = self_attend_back(
        q1, k1, v1, attended_heads, grad_attended, self_lse, self_info, own
    )
    grad_triple_all = jnp.concatenate([from_heads(g) for g in heads_back], 1)
    triple_grad = reduce_weight(in_weight_grad(rows_in, grad_triple_all))
    input_part = in_proj_back(grad_triple_all, triple_w)
    grad_own = (
        e1[:own]
        + input_part[:own]
        + swap_row(input_part[own:].astype(jnp.bfloat16)).astype(jnp.float32)
    )

    def give_tokens(value):
        return regroup(to_features(value.astype(jnp.bfloat16)), back_select, back_place, groups)

    output = give_tokens(final[:own])
    grad_tokens = give_tokens(grad_own)
    sums = lax.psum(
        jnp.stack([gain_one, gain_two, gain_three, bias_one, bias_two, bias_three]),
        ("dp", "row", "col"),
    )
    sums = lax.dynamic_slice_in_dim(sums, col_index * width, width, 1)
    return (
        output,
        grad_tokens,
        grad_passages,
        triple_grad.reshape(triple_weight.shape),
        self_out_grad,
        query_grad.reshape(query_weight.shape),
        memory_grad.reshape(memory_weight.shape),
        cross_out_grad,
        expand_grad.reshape(expand_weight.shape),
        contract_grad,
        sums[:3],
        sums[3:],
    )


def solution(mesh):
    in_specs = (
        P(("dp", "row"), "col"),
        P(("dp", "row"), None, "col"),
        P(),
        P(),
        P(),
        P("col", None, "row"),
        P("row", "col"),
        P("col", None, "row"),
        P("col", None, "row"),
        P("row", "col"),
        P("col", None, "row"),
        P("row", "col"),
        P(None, "col"),
        P(None, "col"),
        P(("dp", "row"), "col"),
    )
    out_specs = (
        P(("dp", "row"), "col"),
        P(("dp", "row"), "col"),
        P(("dp", "row"), None, "col"),
        P("col", None, "row"),
        P("row", "col"),
        P("col", None, "row"),
        P("col", None, "row"),
        P("row", "col"),
        P("col", None, "row"),
        P("row", "col"),
        P(None, "col"),
        P(None, "col"),
    )
    return jax.shard_map(
        on_device, mesh=mesh, in_specs=in_specs, out_specs=out_specs, check_vma=False
    )
```

time: 2590 us -> 1260 us (0.49)
  waiting for transfers between devices: 1910 us -> 603 us
  matrix products: 253 us -> 76.3 us
  other arithmetic: 172 us -> 62.7 us
  Pallas kernels: 0 us -> 106 us
  blocking collectives: 103 us -> 177 us
  starting transfers between devices: 14.1 us -> 86.5 us
    reduce_scatter x12 -> x8, waiting for transfers between devices: 975 us -> 169 us  [the longest x7 169 us: reduce_weight(): lax.psum_scatter(flat, ('col', 'dp'), scatter_dimension=0, tiled=True)]
    all_gather x14 -> x10, waiting for transfers between devices: 754 us -> 140 us  [the longest x3 64.8 us: gather_out(): return lax.all_gather(weight, 'col', axis=0, tiled=False)]
    dot_general x77 -> x21, matrix products: 253 us -> 76.3 us  [the longest x4 16.4 us: in_proj_back(): jnp.einsum('te,fe->tf', grad, weight, preferred_element_type=jnp.float32)]
    all_to_all x3 -> x16, waiting for transfers between devices: 24.5 us -> 195 us  [the longest x7 88.7 us: to_features(): lax.all_to_all(parts, 'col', 0, 0, tiled=True)]
    pallas_call x0 -> x4, Pallas kernels: none -> 106 us  [the longest x1 36.2 us: cross_attend_back(): pl.pallas_call(lambda *refs: cross_backward_kernel(passages, span, valid,...]
    ppermute x0 -> x15, waiting for transfers between devices: none -> 94.9 us  [swap_row(): return lax.ppermute(value, 'row', [(0, 1), (1, 0)])]
    convert_element_type x23 -> x8, other arithmetic: 102 us -> 18 us  [the longest x1 10.2 us: on_device(): active = active.astype(jnp.bfloat16)]
    unnamed x31 -> x18, waiting for transfers between devices: 87.5 us -> 4.27 us
  transfers between devices with their start and end apart: 32 -> 49, of which waited for: 29 -> 34; matrix products, arithmetic and copies ran while one was open for 4% -> 17% of each run, Pallas kernels for 0% -> 9%
where the time goes in v1:
time: 1260 us; the launch traced here: 1250 us
  waiting for transfers between devices  603 us (48%)
  blocking collectives  177 us (14%)
  local copies, waits for them, and re-layouts  121 us (10%)
  Pallas kernels  106 us (8%)
  starting transfers between devices  86.5 us (7%)
  matrix products  76.3 us (6%)
  other arithmetic  62.7 us (5%)
  between operations  16.1 us (1%)
    reduce_scatter x7, waiting for transfers between devices, reduce_weight(): lax.psum_scatter(flat, ('col', 'dp'), scatter_dimension=0, tiled=True)  169 us
    ppermute x15, waiting for transfers between devices, swap_row(): return lax.ppermute(value, 'row', [(0, 1), (1, 0)])  94.9 us
    all_to_all x7, waiting for transfers between devices, to_features(): lax.all_to_all(parts, 'col', 0, 0, tiled=True)  88.7 us
    all_to_all x5, waiting for transfers between devices, to_tokens(): lax.all_to_all(rows.reshape(cols, count // cols, width), 'col', 0, 0, til...  79.1 us
    all_gather x3, waiting for transfers between devices, gather_out(): return lax.all_gather(weight, 'col', axis=0, tiled=False)  64.8 us
    all_to_all x2, blocking collectives, to_tokens(): lax.all_to_all(rows.reshape(cols, count // cols, width), 'col', 0, 0, til...  58.6 us
    all_gather x4, waiting for transfers between devices, gather_in(): return lax.all_gather(weight, 'col', axis=0, tiled=True)  45 us
    all_gather x5, blocking collectives, reduce_weight(): return lax.all_gather(part, 'dp', axis=0, tiled=True).astype(jnp.float32)  43.7 us
  transfers between devices with their start and end apart: 49, of which 34 were waited for; matrix products, arithmetic and copies ran while one was open for 17% of the time, Pallas kernels for 9%

profile of v1, /device:TPU:0, one launch (start us, length us, event | category | flops | bytes accessed | tf_op | source)
XLA Modules:
  0.0 1249.2 jit_solution(2642747148004266130)
XLA Ops:
  19.2 32.7 %all-to-all-done.6 = bf16[4,300,256]{2,1,0:T(8,128)(2,1)S(1)} async-done(((bf16[4,300,256]{2,1,0:T(8,128)(2,1)}), bf16[4,300,256]{2,1,0:T(8,128)(2,1)S(1)}, u32[]{:S(2)}, u32[]{:S(2)}) %all-to-all-start.6) | async-done | bytes 614432 | tf_op jit(solution)/shard_map/all_to_all | solution.py:29
  83.2 13.7 %all-to-all-done = bf16[16,128,256]{2,1,0:T(8,128)(2,1)S(1)} async-done(((bf16[16,128,256]{2,1,0:T(8,128)(2,1)}), bf16[16,128,256]{2,1,0:T(8,128)(2,1)S(1)}, u32[]{:S(2)}, u32[]{:S(2)}) %all-to-all-start) | async-done | bytes 1048608 | tf_op jit(solution)/shard_map/all_to_all | solution.py:51
  97.5 30.5 %all_to_all.90 = bf16[4,256,256]{2,1,0:T(8,128)(2,1)S(1)} all-to-all(bf16[4,256,256]{2,1,0:T(8,128)(2,1)S(1)} %bitcast.360), channel_id=1, replica_groups=mesh['dp'=4,'row'=2,'col'=4] {'col'}, dimensions={0} | all-to-all | bytes 1048576 | tf_op jit(solution)/shard_map/all_to_all | solution.py:29
  129.0 14.0 %collective-permute-done = bf16[256,1024]{1,0:T(8,128)(2,1)S(1)} collective-permute-done((bf16[256,1024]{1,0:T(8,128)(2,1)S(1)}, bf16[256,1024]{1,0:T(8,128)(2,1)S(1)}, u32[]{:S(2)}, u32[]{:S(2)}) %collective-permute-start) | collective-permute-done | bytes 524320 | tf_op jit(solution)/shard_map/ppermute | solution.py:23
  155.6 25.6 %all-to-all-done.2 = bf16[4,512,128]{2,1,0:T(8,128)(2,1)S(1)} async-done(((bf16[4,512,128]{2,1,0:T(8,128)(2,1)}), bf16[4,512,128]{2,1,0:T(8,128)(2,1)S(1)}, u32[]{:S(2)}, u32[]{:S(2)}) %all-to-all-start.2) | async-done | bytes 524320 | tf_op jit(solution)/shard_map/all_to_all | solution.py:37
  203.3 23.2 %all-to-all-done.4 = bf16[4,512,128]{2,1,0:T(8,128)(2,1)S(1)} async-done(((bf16[4,512,128]{2,1,0:T(8,128)(2,1)}), bf16[4,512,128]{2,1,0:T(8,128)(2,1)S(1)}, u32[]{:S(2)}, u32[]{:S(2)}) %all-to-all-start.4) | async-done | bytes 524320 | tf_op jit(solution)/shard_map/all_to_all | solution.py:37
  227.3 18.9 %self_attend.1 = (bf16[2048,128]{1,0:T(8,128)(2,1)}, f32[8,1,512]{2,1,0:T(1,128)}) custom-call(s32[9]{0:T(128)} %pad_add_fusion.1.refs_0_, bf16[2048,128]{1,0:T(8,128)(2,1)} %bitcast.371, bf16[2048,128]{1,0:T(8,128)(2,1)} %bitcast.373, bf16[2048,128]{1,0:T(8,128)(2,1)} %bitcast.375), custom_call_target="tpu_custom_call" | custom-call | flops 4294967296 | bytes 2097152 | tf_op jit(solution)/shard_map/self_attend/pallas_call | solution.py:310
  251.5 34.2 %all_gather.60 = bf16[6,1024]{1,0:T(8,128)(2,1)S(1)} all-gather(bf16[6,256]{1,0:T(8,128)(2,1)S(1)} %pad_maximum_fusion.7), channel_id=1, replica_groups=mesh['dp'=4,'row'=2,'col'=4] {'col'}, dimensions={1}, use_global_device_ids=true | all-gather | bytes 15360 | tf_op jit(solution)/shard_map/all_gather | solution.py:603
  343.7 26.3 %cross_attend.1 = (bf16[512,512]{1,0:T(8,128)(2,1)}, f32[4,2,1,512]{3,2,1,0:T(1,128)}) custom-call(s32[28]{0:T(128)} %pad_add_fusion.2.refs_0_, bf16[512,512]{1,0:T(8,128)(2,1)} %convolution_convert_fusion.8.refs_1_, bf16[2432,1024]{1,0:T(8,128)(2,1)} %all-gather.20.cloned.1.call-done.refs_2_.refs_3_, ...), custom_call_target="tpu_custom_call" | custom-call | flops 10200547328 | bytes 4980736 | tf_op jit(solution)/shard_map/cross_attend/pallas_call | solution.py:453
  393.0 19.7 %collective-permute-done.5 = bf16[256,1024]{1,0:T(8,128)(2,1)} collective-permute-done((bf16[256,1024]{1,0:T(8,128)(2,1)}, bf16[256,1024]{1,0:T(8,128)(2,1)}, u32[]{:S(2)}, u32[]{:S(2)}) %collective-permute-start.5) | collective-permute-done | bytes 524320 | tf_op jit(solution)/shard_map/ppermute | solution.py:23
  416.8 36.4 %all-gather.32.cloned.1.call-done = bf16[1024,1,2048]{2,0,1:T(8,128)(2,1)} async-done(((bf16[256,1,2048]{2,0,1:T(8,128)(2,1)}), bf16[1024,1,2048]{2,0,1:T(8,128)(2,1)}) %all-gather.32.cloned.1.call-update) | async-done | bytes 4194320 | tf_op jit(solution)/shard_map/all_gather | solution.py:56
  470.6 63.4 %all-gather.34.cloned.1.call-done = bf16[8192,256]{1,0:T(8,128)(2,1)} async-done(((bf16[2048,256]{1,0:T(8,128)(2,1)}), bf16[8192,256]{1,0:T(8,128)(2,1)}) %all-gather.34.cloned.1.call-update) | async-done | bytes 4194320 | tf_op jit(solution)/shard_map/all_gather | solution.py:60
  644.6 36.2 %cross_attend_back.1 = (bf16[512,512]{1,0:T(8,128)(2,1)}, bf16[2432,1024]{1,0:T(8,128)(2,1)}) custom-call(s32[28]{0:T(128)} %pad_add_fusion.2.refs_0_, bf16[512,512]{1,0:T(8,128)(2,1)} %convolution_convert_fusion.8.refs_1_, bf16[2432,1024]{1,0:T(8,128)(2,1)} %all-gather.20.cloned.1.call-done.refs_2_.refs_3_, ...), custom_call_target="tpu_custom_call" | custom-call | flops 25501368320 | bytes 14942208 | tf_op jit(solution)/shard_map/cross_attend_back/pallas_call | solution.py:483
  731.8 14.8 %all-to-all-done.11 = bf16[4,512,128]{2,1,0:T(8,128)(2,1)S(1)} async-done(((bf16[4,512,128]{2,1,0:T(8,128)(2,1)}), bf16[4,512,128]{2,1,0:T(8,128)(2,1)S(1)}, u32[]{:S(2)}, u32[]{:S(2)}) %all-to-all-start.11) | async-done | bytes 524320 | tf_op jit(solution)/shard_map/all_to_all | solution.py:37
  747.4 24.8 %self_attend_back.1 = (bf16[2048,128]{1,0:T(8,128)(2,1)}, bf16[2048,128]{1,0:T(8,128)(2,1)}, bf16[2048,128]{1,0:T(8,128)(2,1)}) custom-call(s32[9]{0:T(128)} %pad_add_fusion.1.refs_0_, bf16[2048,128]{1,0:T(8,128)(2,1)} %bitcast.372, bf16[2048,128]{1,0:T(8,128)(2,1)} %bitcast.374, bf16[2048,128]{1,0:T(8,128)(2,1)} %bitcast.376, ...), custom_call_target="tpu_custom_call" | custom-call | flops 10737418240 | bytes 4194304 | tf_op jit(solution)/shard_map/self_attend_back/pallas_call | solution.py:336
  779.9 24.6 %all-to-all-done.12 = bf16[4,512,128]{1,2,0:T(8,128)(2,1)S(1)} async-done(((bf16[4,512,128]{1,2,0:T(8,128)(2,1)}), bf16[4,512,128]{1,2,0:T(8,128)(2,1)S(1)}, u32[]{:S(2)}, u32[]{:S(2)}) %all-to-all-start.12) | async-done | bytes 524320 | tf_op jit(solution)/shard_map/all_to_all | solution.py:29
  816.8 21.8 %all-to-all-done.13 = bf16[4,512,128]{1,2,0:T(8,128)(2,1)} async-done(((bf16[4,512,128]{1,2,0:T(8,128)(2,1)}), bf16[4,512,128]{1,2,0:T(8,128)(2,1)}, u32[]{:S(2)}, u32[]{:S(2)}) %all-to-all-start.13) | async-done | bytes 524320 | tf_op jit(solution)/shard_map/all_to_all | solution.py:29
  838.6 28.1 %all_to_all.91 = bf16[4,512,128]{1,2,0:T(8,128)(2,1)S(1)} all-to-all(bf16[4,512,128]{1,2,0:T(8,128)(2,1)} %copy.269), channel_id=1, replica_groups=mesh['dp'=4,'row'=2,'col'=4] {'col'}, dimensions={0} | all-to-all | bytes 1048576 | tf_op jit(solution)/shard_map/all_to_all | solution.py:29
  940.8 16.6 %all_gather.73 = bf16[512,256]{1,0:T(8,128)(2,1)S(1)} all-gather(bf16[128,256]{1,0:T(8,128)(2,1)} %reduce-scatter.19.cloned.1.call-done), channel_id=1, replica_groups=mesh['dp'=4,'row'=2,'col'=4] {'dp'}, dimensions={0}, use_global_device_ids=true | all-gather | bytes 327680 | tf_op jit(solution)/shard_map/all_gather | solution.py:102
  958.3 37.9 %reduce-scatter.15.cloned.1.call-done = bf16[64,512]{1,0:T(8,128)(2,1)} async-done(((bf16[1024,512]{1,0:T(8,128)(2,1)}), bf16[64,512]{1,0:T(8,128)(2,1)}) %reduce-scatter.15.cloned.1.call-update) | async-done | bytes 65552 | tf_op jit(solution)/shard_map/reduce_scatter | solution.py:101
  1003.6 52.7 %reduce-scatter.13.cloned.1.call-done = bf16[128,256]{1,0:T(8,128)(2,1)} async-done(((bf16[2048,256]{1,0:T(8,128)(2,1)}), bf16[128,256]{1,0:T(8,128)(2,1)}) %reduce-scatter.13.cloned.1.call-update) | async-done | bytes 65552 | tf_op jit(solution)/shard_map/reduce_scatter | solution.py:101
  1063.2 40.6 %psum.7 = f32[6,1024]{1,0:T(8,128)S(1)} all-reduce(f32[6,1024]{1,0:T(8,128)S(1)} %stack.27), channel_id=1, replica_groups=mesh['dp'=4,'row'=2,'col'=4] {'dp','row','col'}, use_global_device_ids=true, to_apply=%region_35.36 | all-reduce | flops 6144 | bytes 49152 | tf_op jit(solution)/shard_map/psum | solution.py:684
  1113.2 17.1 %reduce-scatter.11.cloned.1.call-done = bf16[64,1536]{1,0:T(8,128)(2,1)} async-done(((bf16[1024,1536]{1,0:T(8,128)(2,1)}), bf16[64,1536]{1,0:T(8,128)(2,1)}) %reduce-scatter.11.cloned.1.call-update) | async-done | bytes 196624 | tf_op jit(solution)/shard_map/reduce_scatter | solution.py:101
  1171.6 61.5 %reduce-scatter.17.cloned.1.call-done = bf16[64,1024]{1,0:T(8,128)(2,1)} async-done(((bf16[1024,1024]{1,0:T(8,128)(2,1)}), bf16[64,1024]{1,0:T(8,128)(2,1)}) %reduce-scatter.17.cloned.1.call-update) | async-done | bytes 131088 | tf_op jit(solution)/shard_map/reduce_scatter | solution.py:101
  (471 shorter events, 517.8 us)
Async XLA Ops:
  7.2 62.2 %all-gather.18.cloned.1.call-start = ((), (), s32[]{:S(2)}) async-start(), calls=%async_computation.27 | async-start | bytes 2621440 | tf_op jit(solution)/shard_map/all_gather | solution.py:56
  9.3 136.5 %all-gather.16.cloned.1.call-start = ((), (), s32[]{:S(2)}) async-start(), calls=%async_computation.26 | async-start | bytes 3932160 | tf_op jit(solution)/shard_map/all_gather | solution.py:56
  10.6 281.4 %all-gather.26.cloned.1.call-start = ((), (), s32[]{:S(2)}) async-start(), calls=%async_computation.39 | async-start | bytes 1310720 | tf_op jit(solution)/shard_map/all_gather | solution.py:60
  18.6 314.1 %all-gather.28.cloned.1.call-start = ((), (), s32[]{:S(2)}) async-start(), calls=%async_computation.40 | async-start | bytes 1310720 | tf_op jit(solution)/shard_map/all_gather | solution.py:56
  19.1 324.6 %all-gather.20.cloned.1.call-start = ((), (), s32[]{:S(2)}) async-start(), calls=%async_computation.28 | async-start | bytes 6225920 | tf_op jit(solution)/shard_map/all_gather | solution.py:620
  73.6 297.9 %all-gather.30.cloned.1.call-start = ((), (), s32[]{:S(2)}) async-start(), calls=%async_computation.41 | async-start | bytes 1310720 | tf_op jit(solution)/shard_map/all_gather | solution.py:60
  74.1 379.1 %all-gather.32.cloned.1.call-start = ((), (), s32[]{:S(2)}) async-start(), calls=%async_computation.42 | async-start | bytes 5242880 | tf_op jit(solution)/shard_map/all_gather | solution.py:56
  185.1 349.0 %all-gather.34.cloned.1.call-start = ((), (), s32[]{:S(2)}) async-start(), calls=%async_computation.43 | async-start | bytes 5242880 | tf_op jit(solution)/shard_map/all_gather | solution.py:60
  246.1 40.2 %all-to-all-start.5 = ((bf16[4,512,128]{2,1,0:T(8,128)(2,1)}), bf16[4,512,128]{2,1,0:T(8,128)(2,1)S(1)}, u32[]{:S(2)}, u32[]{:S(2)}) async-start(bf16[4,512,128]{2,1,0:T(8,128)(2,1)} %bitcast.377), calls=%async_computation.5 | async-start | bytes 1048576 | tf_op jit(solution)/shard_map/all_to_all | solution.py:29
  307.7 70.5 %all-to-all-start.10 = ((bf16[4,256,256]{2,1,0:T(8,128)(2,1)}), bf16[4,256,256]{2,1,0:T(8,128)(2,1)}, u32[]{:S(2)}, u32[]{:S(2)}) async-start(bf16[4,256,256]{2,1,0:T(8,128)(2,1)} %bitcast.355), calls=%async_computation.10 | async-start | bytes 1048576 | tf_op jit(solution)/shard_map/all_to_all | solution.py:29
  313.3 559.0 %reduce-scatter.21.cloned.1.call-start = ((), (), s32[]{:S(2)}) async-start(), calls=%async_computation.35 | async-start | bytes 4456448 | tf_op jit(solution)/shard_map/reduce_scatter | solution.py:101
  380.1 165.1 %collective-permute-start.8 = (bf16[256,1024]{1,0:T(8,128)(2,1)}, bf16[256,1024]{1,0:T(8,128)(2,1)}, u32[]{:S(2)}, u32[]{:S(2)}) collective-permute-start(bf16[256,1024]{1,0:T(8,128)(2,1)} %bitcast.135), channel_id=1, source_target_pairs={{0,4},{4,0},{1,5},{5,1},{2,6},{6,2},{3,7},{7,3},{8,12},{12,8},{9,1... | collective-permute-start | bytes 1572872 | tf_op jit(solution)/shard_map/ppermute | solution.py:23
  590.2 282.7 %reduce-scatter.23.cloned.1.call-start = ((), (), s32[]{:S(2)}) async-start(), calls=%async_computation.37 | async-start | bytes 4456448 | tf_op jit(solution)/shard_map/reduce_scatter | solution.py:101
  603.3 295.8 %reduce-scatter.9.cloned.1.call-start = ((), (), s32[]{:S(2)}) async-start(), calls=%async_computation.29 | async-start | bytes 6225920 | tf_op jit(solution)/shard_map/reduce_scatter | solution.py:651
  680.8 260.1 %reduce-scatter.19.cloned.1.call-start = ((), (), s32[]{:S(2)}) async-start(), calls=%async_computation.34 | async-start | bytes 1114112 | tf_op jit(solution)/shard_map/reduce_scatter | solution.py:101
  730.1 266.2 %reduce-scatter.15.cloned.1.call-start = ((), (), s32[]{:S(2)}) async-start(), calls=%async_computation.32 | async-start | bytes 1114112 | tf_op jit(solution)/shard_map/reduce_scatter | solution.py:101
  809.3 247.0 %reduce-scatter.13.cloned.1.call-start = ((), (), s32[]{:S(2)}) async-start(), calls=%async_computation.31 | async-start | bytes 1114112 | tf_op jit(solution)/shard_map/reduce_scatter | solution.py:101
  814.6 315.7 %reduce-scatter.11.cloned.1.call-start = ((), (), s32[]{:S(2)}) async-start(), calls=%async_computation.30 | async-start | bytes 3342336 | tf_op jit(solution)/shard_map/reduce_scatter | solution.py:101
  872.2 277.3 %all-gather.22.cloned.1.call-start = ((), (), s32[]{:S(2)}) async-start(), calls=%async_computation.36 | async-start | bytes 1310720 | tf_op jit(solution)/shard_map/all_gather | solution.py:102
  872.8 294.9 %all-gather.24.cloned.1.call-start = ((), (), s32[]{:S(2)}) async-start(), calls=%async_computation.38 | async-start | bytes 1310720 | tf_op jit(solution)/shard_map/all_gather | solution.py:102
  899.0 334.1 %reduce-scatter.17.cloned.1.call-start = ((), (), s32[]{:S(2)}) async-start(), calls=%async_computation.33 | async-start | bytes 2228224 | tf_op jit(solution)/shard_map/reduce_scatter | solution.py:101
  923.8 181.4 %collective-permute-start.14 = (bf16[304,1024]{1,0:T(8,128)(2,1)S(1)}, bf16[304,1024]{1,0:T(8,128)(2,1)}, u32[]{:S(2)}, u32[]{:S(2)}) collective-permute-start(bf16[304,1024]{1,0:T(8,128)(2,1)S(1)} %slice.372), channel_id=1, source_target_pairs={{0,4},{4,0},{1,5},{5,1},{2,6},{6,2},{3,7},{7,3},{8,12},{12,8},{9,1... | collective-permute-start | bytes 1867784 | tf_op jit(solution)/shard_map/ppermute | solution.py:23
  937.3 170.4 %all-to-all-start.16 = ((bf16[16,128,256]{2,1,0:T(8,128)(2,1)}), bf16[16,128,256]{2,1,0:T(8,128)(2,1)S(1)}, u32[]{:S(2)}, u32[]{:S(2)}) async-start(bf16[16,128,256]{2,1,0:T(8,128)(2,1)} %gather_fusion.8), calls=%async_computation.16 | async-start | bytes 2097152 | tf_op jit(solution)/shard_map/all_to_all | solution.py:51
  1107.7 62.8 %all-to-all-start.17 = ((bf16[4,300,256]{2,1,0:T(8,128)(2,1)}), bf16[4,300,256]{2,1,0:T(8,128)(2,1)S(1)}, u32[]{:S(2)}, u32[]{:S(2)}) async-start(bf16[4,300,256]{2,1,0:T(8,128)(2,1)} %bitcast.286), calls=%async_computation.18 | async-start | bytes 1245184 | tf_op jit(solution)/shard_map/all_to_all | solution.py:37
  (110 other events, 1410.0 us)
Sparse Core Ops, SparseCore 0:
  10.2 59.2 all-gather.17
  71.6 74.2 all-gather.15
  147.4 38.3 all-gather.25
  187.2 39.6 all-gather.27
  228.8 114.8 all-gather.19
  345.2 26.2 all-gather.29
  373.0 80.1 all-gather.31
  454.8 79.2 all-gather.33
  590.4 71.4 reduce-scatter.20
  665.6 75.5 reduce-scatter.22
  743.5 114.3 reduce-scatter.8
  861.4 74.0 reduce-scatter.18
  939.2 57.0 reduce-scatter.14
  999.7 56.5 reduce-scatter.12
  1059.9 70.3 reduce-scatter.10
  1131.7 17.7 all-gather.21
  1151.0 16.6 all-gather.23
  1171.3 61.7 reduce-scatter.16
